TPU v7x, 512 devices: a whole 4x4x16 slice. The times are simulated.
512 devices in a mesh: lat: 4 (over x_hi, core), lon: 32 (over z, x_lo), tensor: 4 (over y).
Axes of the slice: x: 4 (x_hi: 2, x_lo: 2; x = x_hi * 2 + x_lo), y: 4, z: 16, core: 2. Of those that a mesh axis runs over, the one named last changes fastest.
Arguments:
- fields: bfloat16 [64, 768, 256], P('lat', 'lon'), may hold values from -8 to 8
- norm_gain1: float32 [256], replicated, may hold values from 0.5 to 1.5
- w_qkv: bfloat16 [256, 3, 8, 32], P(None, None, 'tensor'), may hold values from -0.1875 to 0.1875
- logit_scale: float32 [8], P('tensor'), may hold values from 1 to 64
- w_out: bfloat16 [8, 32, 256], P('tensor'), may hold values from -0.375 to 0.375
- attn_keep: int32 [64, 256], P('lat'), may hold values 0 or 1
- dw_kernel: bfloat16 [7, 7, 256], replicated, may hold values from -0.875 to 0.875
- norm_gain2: float32 [256], replicated, may hold values from 0.5 to 1.5
- w_up: bfloat16 [256, 1024], P(None, 'tensor'), may hold values from -0.375 to 0.375
- w_down: bfloat16 [1024, 256], P('tensor'), may hold values from -0.1875 to 0.1875
- mlp_keep: int32 [64, 256], P('lat'), may hold values 0 or 1
Outputs:
- result: bfloat16 [64, 768, 256], P('lat', 'lon')
All inputs are finite; a program needn't handle non-finite values. No bound on the sum of `attn_keep` or of `mlp_keep` on one device may be relied on, other than what follows from the above.
Results may differ from a plain program's by a relative error of at most 0.014.
Values may be sent and summed in bfloat16 or wider, within the bound.
A program may use at most 64 MiB of HBM per device.

v0:
```python
import math

import jax
import jax.numpy as jnp
from jax import lax
from jax.sharding import PartitionSpec as P

ln_eps = 1e-05
keep_prob = 0.9


def padded(shard, sides, width, wrap):
    for axis, dim in sides:
        size, length = (lax.axis_size(axis), shard.shape[dim])
        up = [(i, (i + 1) % size) for i in range(size if wrap else size - 1)]
        down = [(j, i) for i, j in up]
        last = lax.slice_in_dim(shard, length - width, length, axis=dim)
        first = lax.slice_in_dim(shard, 0, width, axis=dim)
        before = lax.ppermute(last, axis, up)
        after = lax.ppermute(first, axis, down)
        shard = jnp.concatenate([before, shard, after], axis=dim)
    return shard


def layer_norm(values, gain):
    widened = values.astype(jnp.float32)
    center = jnp.mean(widened, axis=-1, keepdims=True)
    spread = jnp.mean(jnp.square(widened - center), axis=-1, keepdims=True)
    return (widened - center) * lax.rsqrt(spread + ln_eps) * gain


def depthwise(wide, kernel, rows, cols):
    kernel_f = kernel.astype(jnp.float32)
    wide_f = wide.astype(jnp.float32)
    width = kernel.shape[0]
    total = jnp.zeros((rows, cols, wide.shape[2]), jnp.float32)
    for row_off in range(width):
        for col_off in range(width):
            total = (
                total
                + kernel_f[row_off, col_off]
                * wide_f[row_off : row_off + rows, col_off : col_off + cols]
            )
    return total


def widen(stream, margin):
    rows_wide = padded(stream, (("lat", 0),), margin, False)
    return padded(rows_wide, (("lon", 1),), margin, True)


def feed_forward(spatial, norm_gain2, w_up, w_down):
    normed2 = layer_norm(spatial, norm_gain2).astype(jnp.bfloat16)
    hidden = jax.nn.gelu(
        jnp.einsum("rlc,cf->rlf", normed2, w_up, preferred_element_type=jnp.float32),
        approximate=False,
    ).astype(jnp.bfloat16)
    return jnp.einsum("rlf,fc->rlc", hidden, w_down, preferred_element_type=jnp.float32)


def shards(
    fields,
    norm_gain1,
    w_qkv,
    logit_scale,
    w_out,
    attn_keep,
    dw_kernel,
    norm_gain2,
    w_up,
    w_down,
    mlp_keep,
):
    lat_rows, lon_cols, channels = fields.shape
    local_heads = w_qkv.shape[2]
    head_size = w_qkv.shape[3]
    logit_coef = logit_scale * (1.0 / math.sqrt(head_size))
    normed = layer_norm(fields, norm_gain1).astype(jnp.bfloat16)
    projected = jnp.einsum(
        "rlc,cjhd->rljhd", normed, w_qkv, preferred_element_type=jnp.float32
    ).astype(jnp.bfloat16)
    queries = projected[:, :, 0]
    keys_values = projected[:, :, 1:].reshape(lat_rows, lon_cols, 2 * local_heads * head_size)
    piece = lax.all_gather(keys_values, "lon", axis=1, tiled=True)
    running_max = jnp.full((lat_rows, local_heads, lon_cols), -1e30, jnp.float32)
    count = piece.shape[1]
    split_piece = piece.reshape(lat_rows, count, 2, local_heads, head_size)
    scores = jnp.einsum(
        "rqhd,rkhd->rhqk", queries, split_piece[:, :, 0], preferred_element_type=jnp.float32
    )
    scores = scores * logit_coef[None, :, None, None]
    new_max = jnp.maximum(running_max, jnp.max(scores, axis=-1))
    weights = jnp.exp(scores - new_max[..., None])
    new_sum = jnp.sum(weights, axis=-1)
    gathered = jnp.einsum(
        "rhqk,rkhd->rhqd",
        weights.astype(jnp.bfloat16),
        split_piece[:, :, 1],
        preferred_element_type=jnp.float32,
    )
    mixed = (gathered / new_sum[..., None]).astype(jnp.bfloat16)
    partial_value = jnp.einsum("rhqd,hdc->rqc", mixed, w_out, preferred_element_type=jnp.float32)
    attended = lax.psum(partial_value.astype(jnp.bfloat16), "tensor").astype(jnp.float32)
    attn_factor = (attn_keep.astype(jnp.float32) / keep_prob)[:, None, :]
    mlp_factor = (mlp_keep.astype(jnp.float32) / keep_prob)[:, None, :]
    margin = dw_kernel.shape[0] // 2
    stream = (fields.astype(jnp.float32) + attended * attn_factor).astype(jnp.bfloat16)
    spatial = depthwise(widen(stream, margin), dw_kernel, lat_rows, lon_cols).astype(jnp.bfloat16)
    ffn_sum = lax.psum(
        feed_forward(spatial, norm_gain2, w_up, w_down).astype(jnp.bfloat16), "tensor"
    ).astype(jnp.float32)
    result = (stream.astype(jnp.float32) + ffn_sum * mlp_factor).astype(jnp.bfloat16)
    return result


def solution(mesh):
    placed = (
        P("lat", "lon", None),
        P(),
        P(None, None, "tensor", None),
        P("tensor"),
        P("tensor", None, None),
        P("lat", None),
        P(),
        P(),
        P(None, "tensor"),
        P("tensor", None),
        P("lat", None),
    )
    return jax.shard_map(
        shards, mesh=mesh, in_specs=placed, out_specs=P("lat", "lon", None), check_vma=False
    )
```

profile of v0, /device:TPU:4, one launch (start us, length us, event | category | flops | bytes accessed | tf_op | source)
XLA Modules:
  0.0 309.5 jit_solution(4489916328786344057)
XLA Ops:
  6.5 1.1 convert_reduce_fusion
  7.7 1.2 fusion.18
  8.8 1.4 convolution_convert_fusion
  10.3 0.3 copy.12
  10.6 0.9 reshape.39
  11.6 141.9 %all-gather.2.cloned.1.call-done = bf16[16,768,128]{2,1,0:T(8,128)(2,1)} async-done(((bf16[16,24,128]{2,1,0:T(8,128)(2,1)}), bf16[16,768,128]{2,1,0:T(8,128)(2,1)}) %all-gather.2.cloned.1.call-update) | async-done | bytes 3145744 | tf_op jit(solution)/shard_map/all_gather | solution.py:84
  153.5 4.7 %copy.13 = bf16[16,768,128]{1,2,0:T(8,128)(2,1)} copy(bf16[16,768,128]{2,1,0:T(8,128)(2,1)} %all-gather.2.cloned.1.call-done) | data formatting | bytes 6291456 | tf_op jit(solution)/shard_map/all_gather | solution.py:84
  158.2 2.0 multiply_reduce_fusion
  160.2 0.6 fusion
  160.8 3.2 %fusion.11 = bf16[16,24,256]{2,1,0:T(8,128)(2,1)} fusion(bf16[16,768,2,2,32]{1,4,3,2,0:T(8,128)(2,1)} %bitcast.96, f32[16,2,24,768]{3,2,1,0:T(8,128)S(1)} %get-tuple-element.63, f32[16,2,24]{2,1,0:T(2,128)S(1)} %broadcast_maximum_fusion, f32[2]{0:T(128)S(1)} %broadcast_multiply_fusion.2, f32[16,2,24]{2,1,0:T(2,128)S(1)} %fusion, ...), kind=kOutput, calls=%fused_computation.14 | convolution fusion | flops 52248576 | bytes 4167688 | tf_op jit(solution)/shard_map/rhqd,hdc->rqc/dot_general | solution.py:102
  164.1 53.7 %all-reduce.3.cloned.1.call-done = bf16[16,24,256]{2,1,0:T(8,128)(2,1)} async-done(((bf16[16,24,256]{2,1,0:T(8,128)(2,1)}), bf16[16,24,256]{2,1,0:T(8,128)(2,1)}) %all-reduce.3.cloned.1.call-update) | async-done | bytes 196624 | tf_op jit(solution)/shard_map/psum | solution.py:103
  217.8 1.0 fusion.24
  218.8 1.9 collective-permute-start
  220.8 5.1 %collective-permute-start.1 = (bf16[3,24,256]{2,1,0:T(8,128)(2,1)S(1)}, bf16[3,24,256]{2,1,0:T(8,128)(2,1)S(1)}, u32[]{:S(2)}, u32[]{:S(2)}) collective-permute-start(bf16[3,24,256]{2,1,0:T(8,128)(2,1)S(1)} %get-tuple-element.12), channel_id=1, source_target_pairs={{128,0},{256,128},{384,256},{129,1},{257,129},{385,257},{130,2},{2... | collective-permute-start | bytes 110600 | tf_op jit(solution)/shard_map/ppermute | solution.py:20
  225.9 1.6 collective-permute-done.1
  227.6 3.1 collective-permute-start.2
  230.7 5.4 %collective-permute-start.3 = (bf16[22,3,256]{2,1,0:T(4,128)(2,1)S(1)}, bf16[22,3,256]{2,1,0:T(4,128)(2,1)S(1)}, u32[]{:S(2)}, u32[]{:S(2)}) collective-permute-start(bf16[22,3,256]{2,1,0:T(4,128)(2,1)S(1)} %get-tuple-element.10), channel_id=1, source_target_pairs={{4,0},{8,4},{12,8},{16,12},{20,16},{24,20},{28,24},{32,28},{36,32}... | collective-permute-start | bytes 101384 | tf_op jit(solution)/shard_map/ppermute | solution.py:20
  236.1 1.6 collective-permute-done.3
  237.9 2.9 convert_reduce_fusion.1
  240.8 0.2 fusion.21
  241.1 0.3 fusion.95
  241.5 1.8 convolution_convert_fusion.1
  243.3 58.1 %all-reduce.5.cloned.1.call-done = bf16[16,24,256]{2,1,0:T(8,128)(2,1)} async-done(((bf16[16,24,256]{2,1,0:T(8,128)(2,1)}), bf16[16,24,256]{2,1,0:T(8,128)(2,1)}) %all-reduce.5.cloned.1.call-update) | async-done | bytes 196624 | tf_op jit(solution)/shard_map/psum | solution.py:109
  301.3 1.7 add_convert_fusion
  (41 shorter events, 0.6 us)
Async XLA Ops:
  6.5 234.6 %copy-start = (bf16[256,256]{1,0:T(8,128)(2,1)S(1)}, bf16[256,256]{1,0:T(8,128)(2,1)}, u32[]{:S(2)}) copy-start(bf16[256,256]{1,0:T(8,128)(2,1)} %param.19) | copy-start | bytes 393220
  6.5 5.0 %copy-start.8 = (f32[2]{0:T(128)S(1)}, f32[2]{0:T(128)}, u32[]{:S(2)}) copy-start(f32[2]{0:T(128)} %param.14) | copy-start | bytes 28
  6.5 5.0 %copy-start.3 = (s32[16,256]{1,0:T(8,128)S(1)}, s32[16,256]{1,0:T(8,128)}, u32[]{:S(2)}) copy-start(s32[16,256]{1,0:T(8,128)} %param.16) | copy-start | bytes 49156
  6.5 146.9 %all-gather.2.cloned.1.call-start = ((), (), s32[]{:S(2)}) async-start(), calls=%async_computation | async-start | bytes 3244032 | tf_op jit(solution)/shard_map/all_gather | solution.py:84
  11.5 206.3 %all-reduce.3.cloned.1.call-start = ((), (), s32[]{:S(2)}) async-start(), calls=%async_computation.1 | async-start | bytes 393216 | tf_op jit(solution)/shard_map/psum | solution.py:103
  158.2 2.6 copy-start.6
  160.8 3.3 %copy-start.2 = (bf16[7,7,256]{2,1,0:T(8,128)(2,1)S(1)}, bf16[7,7,256]{2,1,0:T(8,128)(2,1)}, u32[]{:S(2)}) copy-start(bf16[7,7,256]{2,1,0:T(8,128)(2,1)} %param.17) | copy-start | bytes 75268
  160.8 57.0 %copy-start.1 = (bf16[16,24,256]{2,1,0:T(8,128)(2,1)S(1)}, bf16[16,24,256]{2,1,0:T(8,128)(2,1)}, u32[]{:S(2)}) copy-start(bf16[16,24,256]{2,1,0:T(8,128)(2,1)} %param.11) | copy-start | bytes 589828
  164.0 137.3 %all-reduce.5.cloned.1.call-start = ((), (), s32[]{:S(2)}) async-start(), calls=%async_computation.2 | async-start | bytes 393216 | tf_op jit(solution)/shard_map/psum | solution.py:109
  218.8 7.1 %collective-permute-start = (bf16[3,24,256]{2,1,0:T(8,128)(2,1)S(1)}, bf16[3,24,256]{2,1,0:T(8,128)(2,1)S(1)}, u32[]{:S(2)}, u32[]{:S(2)}) collective-permute-start(bf16[3,24,256]{2,1,0:T(8,128)(2,1)S(1)} %get-tuple-element.11), channel_id=1, source_target_pairs={{0,128},{128,256},{256,384},{1,129},{129,257},{257,385},{2,130},{1... | collective-permute-start | bytes 110600 | tf_op jit(solution)/shard_map/ppermute | solution.py:19
  220.8 6.8 %collective-permute-start.1 = (bf16[3,24,256]{2,1,0:T(8,128)(2,1)S(1)}, bf16[3,24,256]{2,1,0:T(8,128)(2,1)S(1)}, u32[]{:S(2)}, u32[]{:S(2)}) collective-permute-start(bf16[3,24,256]{2,1,0:T(8,128)(2,1)S(1)} %get-tuple-element.12), channel_id=1, source_target_pairs={{128,0},{256,128},{384,256},{129,1},{257,129},{385,257},{130,2},{2... | collective-permute-start | bytes 110600 | tf_op jit(solution)/shard_map/ppermute | solution.py:20
  227.6 8.6 %collective-permute-start.2 = (bf16[22,3,256]{2,1,0:T(4,128)(2,1)S(1)}, bf16[22,3,256]{2,1,0:T(4,128)(2,1)S(1)}, u32[]{:S(2)}, u32[]{:S(2)}) collective-permute-start(bf16[22,3,256]{2,1,0:T(4,128)(2,1)S(1)} %get-tuple-element.9), channel_id=1, source_target_pairs={{0,4},{4,8},{8,12},{12,16},{16,20},{20,24},{24,28},{28,32},{32,36}... | collective-permute-start | bytes 101384 | tf_op jit(solution)/shard_map/ppermute | solution.py:19
  230.7 7.1 %collective-permute-start.3 = (bf16[22,3,256]{2,1,0:T(4,128)(2,1)S(1)}, bf16[22,3,256]{2,1,0:T(4,128)(2,1)S(1)}, u32[]{:S(2)}, u32[]{:S(2)}) collective-permute-start(bf16[22,3,256]{2,1,0:T(4,128)(2,1)S(1)} %get-tuple-element.10), channel_id=1, source_target_pairs={{4,0},{8,4},{12,8},{16,12},{20,16},{24,20},{28,24},{32,28},{36,32}... | collective-permute-start | bytes 101384 | tf_op jit(solution)/shard_map/ppermute | solution.py:20
  237.9 3.2 %copy-start.7 = (f32[256]{0:T(256)S(1)}, f32[256]{0:T(256)}, u32[]{:S(2)}) copy-start(f32[256]{0:T(256)} %param.18) | copy-start | bytes 3076
  237.9 3.6 %copy-start.5 = (bf16[256,256]{1,0:T(8,128)(2,1)S(1)}, bf16[256,256]{1,0:T(8,128)(2,1)}, u32[]{:S(2)}) copy-start(bf16[256,256]{1,0:T(8,128)(2,1)} %param.20) | copy-start | bytes 393220
  241.5 1.8 copy-start.4
Sparse Core Ops, SparseCore 0:
  11.6 141.8 all-gather.1
  164.1 53.6 all-reduce.2
  243.4 57.9 all-reduce.4
where the time goes:
time: 310 us
  waiting for transfers between devices  257 us (83%)
  starting transfers between devices  15.6 us (5%)
  between operations  13.4 us (4%)
  other arithmetic  8.84 us (3%)
  matrix products  8.69 us (3%)
  local copies, waits for them, and re-layouts  6.01 us (2%)
    all_gather x1, waiting for transfers between devices, shards(): piece = lax.all_gather(keys_values, 'lon', axis=1, tiled=True)  142 us
    psum x1, waiting for transfers between devices, shards(): lax.psum(feed_forward(spatial, norm_gain2, w_up, w_down).astype(jnp.bfloa...  58.1 us
    psum x1, waiting for transfers between devices, shards(): lax.psum(partial_value.astype(jnp.bfloat16), 'tensor').astype(jnp.float32)  53.7 us
    ppermute x2, starting transfers between devices, padded(): after = lax.ppermute(first, axis, down)  10.5 us
  transfers between devices with their start and end apart: 7, of which 6 were waited for; matrix products, arithmetic and copies ran while one was open for 0% of the time, Pallas kernels for 0%

commit v1 on v0

v1 whole, which is shorter than its diff:
```python
import functools
import math

import jax
import jax.numpy as jnp
from jax import lax
from jax.experimental import pallas as pl
from jax.experimental.pallas import tpu as pltpu
from jax.sharding import PartitionSpec as P

ln_eps = 1e-05
keep_prob = 0.9
LANES = 128
SUB = 8
MESH = pl.DeviceIdType.MESH
f32 = jnp.float32
bf16 = jnp.bfloat16


def layer_norm(values, gain):
    center = jnp.mean(values, axis=-1, keepdims=True)
    shifted = values - center
    spread = jnp.mean(jnp.square(shifted), axis=-1, keepdims=True)
    return (shifted * lax.rsqrt(spread + ln_eps) * gain).astype(bf16)


def kernel(
    n_lat,
    n_lon,
    n_ten,
    fields,
    gain1,
    w_qkv,
    logit_scale,
    w_out,
    attn_keep,
    dw_kernel,
    gain2,
    w_up,
    w_down,
    mlp_keep,
    out,
    proj_w,
    sent,
    got,
    values,
    mixed,
    joined,
    out_w,
    out_wide,
    up_w,
    down_w,
    taps,
    ext,
    ext_f,
    done,
    go_sem,
    send_a,
    recv_a,
    send_b,
    send_b_own,
    recv_b,
    send_w,
    recv_w,
    own_w,
    send_h,
    recv_h,
    send_o,
    recv_o,
):
    rows, cols, channels = fields.shape
    heads = w_qkv.shape[1]
    head_size = w_qkv.shape[2]
    groups = cols // SUB
    quarter = rows // n_ten
    all_heads = heads * n_ten
    size = dw_kernel.shape[0]
    margin = size // 2
    halves = channels // LANES
    bands = n_lat * n_ten

    lat = lax.axis_index("lat")
    lon = lax.axis_index("lon")
    ten = lax.axis_index("tensor")
    band = lat * n_ten + ten

    def band_at(step):
        there = lax.rem(band + step + bands, bands)
        return {"lat": there // n_ten, "tensor": lax.rem(there, n_ten)}

    def lon_at(step):
        return lax.rem(lon + step + n_lon, n_lon)

    def ten_at(step):
        return lax.rem(ten + step, n_ten)

    def far_first(i):
        return n_lon // 2 + ((i + 1) // 2) * (1 - 2 * lax.rem(i, 2))

    barrier = pltpu.get_barrier_semaphore()

    def greet(i, carry):
        pl.semaphore_signal(
            barrier, inc=1, device_id={"lon": lon_at(far_first(i))}, device_id_type=MESH
        )
        return carry

    lax.fori_loop(0, n_lon - 1, greet, 0)
    for step in range(1, n_ten):
        pl.semaphore_signal(
            barrier, inc=1, device_id={"tensor": ten_at(step)}, device_id_type=MESH
        )
    for step in (-1, 1):
        pl.semaphore_signal(barrier, inc=1, device_id=band_at(step), device_id_type=MESH)

    proj_w[...] = jnp.zeros_like(proj_w)
    for head in range(heads):
        for which in range(3):
            proj_w[pl.ds(head * LANES + which * head_size, head_size), :] = w_qkv[which, head]
    normed = layer_norm(fields[...].reshape(rows * cols, channels).astype(f32), gain1[...])
    projected = lax.dot_general(
        normed, proj_w[...], (((1,), (1,)), ((), ())), preferred_element_type=f32
    ).astype(bf16)
    projected = projected.reshape(rows, groups, SUB, heads * LANES)
    for row in range(rows):
        for head in range(heads):
            sent[row * heads + head] = projected[row, :, :, head * LANES : (head + 1) * LANES]

    pl.semaphore_wait(barrier, n_lon - 1 + n_ten - 1 + 2)

    def send_pair(i, carry):
        peer = lon_at(far_first(i))
        pltpu.make_async_remote_copy(
            src_ref=sent.at[peer],
            dst_ref=got.at[:, lon],
            send_sem=send_a,
            recv_sem=recv_a,
            device_id={"lon": peer},
            device_id_type=MESH,
        ).start()
        return carry

    lax.fori_loop(0, n_lon - 1, send_pair, 0)
    pltpu.make_async_copy(sent.at[lon], got.at[:, lon], recv_a).start()

    for step in range(1, n_ten):
        pl.semaphore_signal(
            go_sem, inc=1, device_id={"tensor": ten_at(step)}, device_id_type=MESH
        )
    for step in (-1, 1):
        pl.semaphore_signal(go_sem, inc=1, device_id=band_at(step), device_id_type=MESH)

    pairs_w = ((w_out, out_w), (w_up, up_w), (w_down, down_w))
    weight_copies = []
    for kind, (mine, whole) in enumerate(pairs_w):
        for step in range(1, n_ten):
            copy = pltpu.make_async_remote_copy(
                src_ref=mine,
                dst_ref=whole.at[ten],
                send_sem=send_w.at[kind, step - 1],
                recv_sem=recv_w.at[kind, step - 1],
                device_id={"tensor": ten_at(step)},
                device_id_type=MESH,
            )
            copy.start()
            weight_copies.append(copy)
        pltpu.make_async_copy(mine, whole.at[ten], own_w.at[kind]).start()

    for row_off in range(size):
        line = dw_kernel[row_off].astype(f32)
        for col_off in range(size):
            for half in range(halves):
                taps[half, row_off * size + col_off] = jnp.broadcast_to(
                    line[col_off : col_off + 1, half * LANES : (half + 1) * LANES],
                    (SUB, LANES),
                )

    pltpu.make_async_copy(got, got, recv_a).wait()
    keys = groups * n_lon * SUB
    gathered = got[...].reshape(keys, LANES)
    wide = gathered.astype(f32)
    lane = lax.broadcasted_iota(jnp.int32, (keys, LANES), 1)
    at_keys = (lane >= head_size) & (lane < 2 * head_size)
    queries = jnp.where(at_keys, pltpu.roll(wide, head_size, 1), 0.0).astype(bf16)
    for group in range(groups):
        low, high = group * head_size, (group + 1) * head_size
        shift = (low - 2 * head_size) % LANES
        moved = pltpu.roll(wide, shift, 1) if shift else wide
        inside = (lane >= low) & (lane < high)
        last = LANES if group == groups - 1 else high
        values[group, :, :LANES] = jnp.where(inside, moved, 0.0).astype(bf16)
        values[group, :, LANES:] = jnp.where((lane >= low) & (lane < last), 1.0, 0.0).astype(bf16)
    pair_head = lax.rem(lon, heads)
    pair_row = lon // heads
    scale = logit_scale[0]
    for head in range(1, heads):
        scale = jnp.where(pair_head == head, logit_scale[head], scale)
    coef = scale * (math.log2(math.e) / math.sqrt(head_size))
    span = n_lon * SUB
    total = jnp.zeros((span, 2 * LANES), f32)
    for group in range(groups):
        scores = lax.dot_general(
            queries[group * span : (group + 1) * span],
            gathered,
            (((1,), (1,)), ((), ())),
            preferred_element_type=f32,
        )
        top = jnp.max(scores, axis=-1, keepdims=True)
        weights = jnp.exp2((scores - top) * coef).astype(bf16)
        total = total + jnp.dot(weights, values[group], preferred_element_type=f32)
    mixed[...] = (
        (total[:, :LANES] / total[:, LANES:]).astype(bf16).reshape(n_lon, SUB, LANES)
    )

    owner = pair_row // quarter
    slot_row = lax.rem(pair_row, quarter)
    slot_head = ten * heads + pair_head
    pl.semaphore_wait(go_sem, n_ten - 1 + 2)

    def send_back(i, carry):
        peer = lon_at(far_first(i))
        pltpu.make_async_remote_copy(
            src_ref=mixed.at[peer],
            dst_ref=joined.at[slot_row, slot_head],
            send_sem=send_b,
            recv_sem=recv_b,
            device_id={"lon": peer, "tensor": owner},
            device_id_type=MESH,
        ).start()
        return carry

    lax.fori_loop(0, n_lon - 1, send_back, 0)

    @pl.when(owner == ten)
    def _():
        pltpu.make_async_copy(mixed.at[lon], joined.at[slot_row, slot_head], recv_b).start()

    own_back = pltpu.make_async_remote_copy(
        src_ref=mixed.at[lon],
        dst_ref=joined.at[slot_row, slot_head],
        send_sem=send_b_own,
        recv_sem=recv_b,
        device_id={"tensor": owner},
        device_id_type=MESH,
    )

    @pl.when(owner != ten)
    def _():
        own_back.start()

    out_wide[...] = jnp.zeros_like(out_wide)
    pltpu.make_async_copy(w_out, out_w.at[ten], own_w.at[0]).wait()
    for step in range(1, n_ten):
        weight_copies[step - 1].wait_recv()
    for head in range(all_heads):
        block = out_w[head // heads, head % heads]
        for group in range(groups):
            out_wide[
                pl.ds(head * LANES + group * head_size, head_size),
                pl.ds(group * channels, channels),
            ] = block

    pltpu.make_async_copy(joined, joined, recv_b).wait()
    packed = jnp.concatenate(
        [joined[:, head].reshape(quarter * SUB, LANES) for head in range(all_heads)], axis=-1
    )
    attended = jnp.dot(packed, out_wide[...], preferred_element_type=f32)
    for row in range(quarter):
        at = ten * quarter + row
        factor = attn_keep[pl.ds(at, 1), :].astype(f32) / keep_prob
        block = fields[at].astype(f32)
        for group in range(groups):
            piece = attended[
                row * SUB : (row + 1) * SUB, group * channels : (group + 1) * channels
            ]
            ext[margin + row, pl.ds((group + 1) * SUB, SUB), :] = (
                block[group * SUB : (group + 1) * SUB] + piece * factor
            ).astype(bf16)

    first, final = pl.ds(SUB, SUB), pl.ds(cols, SUB)
    left, right, middle = pl.ds(0, SUB), pl.ds(cols + SUB, SUB), pl.ds(SUB, cols)
    top_rows, low_rows = pl.ds(margin, margin), pl.ds(quarter, margin)
    above, below, own_rows = (
        pl.ds(0, margin),
        pl.ds(margin + quarter, margin),
        pl.ds(margin, quarter),
    )
    halo_copies = []
    for band_step, src_rows, dst_rows in (
        (-1, top_rows, below),
        (1, low_rows, above),
        (0, own_rows, own_rows),
    ):
        for lon_step, src_cols, dst_cols in (
            (-1, first, right),
            (1, final, left),
            (0, middle, middle),
        ):
            if band_step == 0 and lon_step == 0:
                continue
            where = dict(band_at(band_step)) if band_step else {}
            if lon_step:
                where["lon"] = lon_at(lon_step)
            index = len(halo_copies)
            copy = pltpu.make_async_remote_copy(
                src_ref=ext.at[src_rows, src_cols],
                dst_ref=ext.at[dst_rows, dst_cols],
                send_sem=send_h.at[index],
                recv_sem=recv_h.at[index],
                device_id=where,
                device_id_type=MESH,
            )
            copy.start()
            halo_copies.append(copy)
    for copy in halo_copies:
        copy.wait_recv()

    for row in range(quarter + 2 * margin):
        line = ext[row].astype(f32)
        if row < margin:
            line = jnp.where(band > 0, line, 0.0)
        if row >= margin + quarter:
            line = jnp.where(band < bands - 1, line, 0.0)
        for half in range(halves):
            ext_f[half, row] = line[:, half * LANES : (half + 1) * LANES]
    parts = []
    for half in range(halves):
        sums = [jnp.zeros((cols, LANES), f32) for _ in range(quarter)]
        for col_off in range(size):
            tap = [
                jnp.concatenate([taps[half, row_off * size + col_off]] * groups, axis=0)
                for row_off in range(size)
            ]
            for row in range(quarter + 2 * margin):
                line = ext_f[half, row, pl.ds(SUB - margin + col_off, cols), :]
                for i in range(quarter):
                    if 0 <= row - i < size:
                        sums[i] = sums[i] + tap[row - i] * line
        parts.append(jnp.concatenate(sums, axis=0))
    spatial = jnp.concatenate(parts, axis=-1).astype(bf16).astype(f32)

    normed2 = layer_norm(spatial, gain2[...])
    for kind in (1, 2):
        mine, whole = pairs_w[kind]
        pltpu.make_async_copy(mine, whole.at[ten], own_w.at[kind]).wait()
        for step in range(1, n_ten):
            weight_copies[kind * (n_ten - 1) + step - 1].wait_recv()
    ffn = jnp.zeros((quarter * cols, channels), f32)
    for part in range(n_ten):
        inner = jnp.dot(normed2, up_w[part], preferred_element_type=f32)
        hidden = (0.5 * inner * (1.0 + lax.erf(inner * math.sqrt(0.5)))).astype(bf16)
        ffn = ffn + jnp.dot(hidden, down_w[part], preferred_element_type=f32)
    for row in range(quarter):
        factor = mlp_keep[pl.ds(ten * quarter + row, 1), :].astype(f32) / keep_prob
        stream = ext[margin + row, middle, :].astype(f32)
        done[row] = (stream + ffn[row * cols : (row + 1) * cols] * factor).astype(bf16)

    mine = pl.ds(ten * quarter, quarter)
    out_copies = []
    for step in range(1, n_ten):
        copy = pltpu.make_async_remote_copy(
            src_ref=done,
            dst_ref=out.at[mine],
            send_sem=send_o.at[step - 1],
            recv_sem=recv_o.at[step - 1],
            device_id={"tensor": ten_at(step)},
            device_id_type=MESH,
        )
        copy.start()
        out_copies.append(copy)
    own_out = pltpu.make_async_copy(done, out.at[mine], send_o.at[n_ten - 1])
    own_out.start()

    pltpu.make_async_copy(sent.at[: n_lon - 1], sent.at[: n_lon - 1], send_a).wait()
    pltpu.make_async_copy(mixed.at[: n_lon - 1], mixed.at[: n_lon - 1], send_b).wait()

    @pl.when(owner != ten)
    def _():
        own_back.wait_send()

    for copy in weight_copies + halo_copies + out_copies:
        copy.wait_send()
    own_out.wait()
    for copy in out_copies:
        copy.wait_recv()


def shards(sizes, fields, gain1, w_qkv, logit_scale, w_out, attn_keep, dw_kernel, gain2, w_up, w_down, mlp_keep):
    n_lat, n_lon, n_ten = sizes
    rows, cols, channels = fields.shape
    heads, head_size = w_qkv.shape[2:]
    hidden = w_up.shape[1]
    groups, quarter, size = cols // SUB, rows // n_ten, dw_kernel.shape[0]
    margin, halves = size // 2, channels // LANES
    span = quarter + 2 * margin
    vmem = pl.BlockSpec(memory_space=pltpu.VMEM)
    hbm = pl.BlockSpec(memory_space=pl.ANY)
    smem = pl.BlockSpec(memory_space=pltpu.SMEM)
    dma = pltpu.SemaphoreType.DMA
    return pl.pallas_call(
        functools.partial(kernel, n_lat, n_lon, n_ten),
        out_shape=jax.ShapeDtypeStruct(fields.shape, bf16),
        in_specs=[vmem, vmem, vmem, smem, hbm, vmem, vmem, vmem, hbm, hbm, vmem],
        out_specs=hbm,
        scratch_shapes=[
            pltpu.VMEM((heads * LANES, channels), bf16),
            pltpu.VMEM((n_lon, groups, SUB, LANES), bf16),
            pltpu.VMEM((groups, n_lon, SUB, LANES), bf16),
            pltpu.VMEM((groups, groups * n_lon * SUB, 2 * LANES), bf16),
            pltpu.VMEM((n_lon, SUB, LANES), bf16),
            pltpu.VMEM((quarter, heads * n_ten, SUB, LANES), bf16),
            pltpu.VMEM((n_ten,) + w_out.shape, bf16),
            pltpu.VMEM((heads * n_ten * LANES, groups * channels), bf16),
            pltpu.VMEM((n_ten, channels, hidden), bf16),
            pltpu.VMEM((n_ten, hidden, channels), bf16),
            pltpu.VMEM((halves, size * size, SUB, LANES), f32),
            pltpu.VMEM((span, cols + 2 * SUB, channels), bf16),
            pltpu.VMEM((halves, span, cols + 2 * SUB, LANES), f32),
            pltpu.VMEM((quarter, cols, channels), bf16),
            pltpu.SemaphoreType.REGULAR,
            dma, dma, dma, dma, dma,
            dma((3, n_ten - 1)),
            dma((3, n_ten - 1)),
            dma((3,)),
            dma((8,)),
            dma((8,)),
            dma((n_ten,)),
            dma((n_ten - 1,)),
        ],
        compiler_params=pltpu.CompilerParams(
            collective_id=0, has_side_effects=True, vmem_limit_bytes=48 << 20
        ),
    )(
        fields,
        gain1.reshape(1, channels),
        w_qkv.transpose(1, 2, 3, 0),
        logit_scale,
        w_out,
        attn_keep,
        dw_kernel,
        gain2.reshape(1, channels),
        w_up,
        w_down,
        mlp_keep,
    )


def solution(mesh):
    sizes = tuple(mesh.shape[axis] for axis in ("lat", "lon", "tensor"))
    placed = (
        P("lat", "lon", None),
        P(),
        P(None, None, "tensor", None),
        P("tensor"),
        P("tensor", None, None),
        P("lat", None),
        P(),
        P(),
        P(None, "tensor"),
        P("tensor", None),
        P("lat", None),
    )
    return jax.shard_map(
        functools.partial(shards, sizes),
        mesh=mesh,
        in_specs=placed,
        out_specs=P("lat", "lon", None),
        check_vma=False,
    )
```

time: 310 us -> 57.3 us (0.18)
  waiting for transfers between devices: 257 us -> 0 us
  Pallas kernels: 0 us -> 48.9 us
  starting transfers between devices: 15.6 us -> 0 us
  between operations: 13.4 us -> 0.02 us
  other arithmetic: 8.84 us -> 0 us
  matrix products: 8.69 us -> 0 us
    all_gather x1 -> x0, waiting for transfers between devices: 142 us -> none  [shards(): piece = lax.all_gather(keys_values, 'lon', axis=1, tiled=True)]
    psum x2 -> x0, waiting for transfers between devices: 112 us -> none  [the longest x1 58.1 us: shards(): lax.psum(feed_forward(spatial, norm_gain2, w_up, w_down).astype(jnp.bfloa...]
    pallas_call x0 -> x1, Pallas kernels: none -> 48.9 us  [shards(): pl.pallas_call(functools.partial(kernel, n_lat, n_lon, n_ten), out_shape=...]
    ppermute x4 -> x0, starting transfers between devices: 15.6 us -> none  [the longest x2 10.5 us: padded(): after = lax.ppermute(first, axis, down)]
    dot_general x5 -> x0, matrix products: 8.69 us -> none  [the longest x1 3.21 us: shards(): jnp.einsum('rhqd,hdc->rqc', mixed, w_out, preferred_element_type=jnp.floa...]
    unnamed x18 -> x23, local copies, waits for them, and re-layouts: 0.05 us -> 7.94 us
    reduce_sum x5 -> x0, other arithmetic: 5.98 us -> none  [the longest x2 4 us: layer_norm(): center = jnp.mean(widened, axis=-1, keepdims=True)]
    all_gather x1 -> x0, local copies, waits for them, and re-layouts: 4.69 us -> none  [shards(): piece = lax.all_gather(keys_values, 'lon', axis=1, tiled=True)]
  transfers between devices with their start and end apart: 7 -> 0, of which waited for: 6 -> 0; matrix products, arithmetic and copies ran while one was open for 0% -> 0% of each run, Pallas kernels for 0% -> 0%
where the time goes in v1:
time: 57.3 us; the launch traced here: 56.8 us
  Pallas kernels  48.9 us (85%)
  local copies, waits for them, and re-layouts  7.94 us (14%)
    pallas_call x1, Pallas kernels, shards(): pl.pallas_call(functools.partial(kernel, n_lat, n_lon, n_ten), out_shape=...  48.9 us
    unnamed x23, local copies, waits for them, and re-layouts  7.94 us

profile of v1, /device:TPU:4, one launch (start us, length us, event | category | flops | bytes accessed | tf_op | source)
XLA Modules:
  0.0 56.8 jit_solution(3362873427419183234)
XLA Ops:
  0.0 0.0 copy-start.9
  0.0 0.0 copy-start.8
  0.0 0.0 copy-start.10
  0.0 0.7 %copy-done.9 = f32[256]{0:T(256)S(1)} copy-done((f32[256]{0:T(256)S(1)}, f32[256]{0:T(256)}, u32[]{:S(2)}) %copy-start.9) | copy-done | bytes 1048
  0.7 0.0 copy-done.8
  0.7 0.0 copy-done.10
  0.7 0.0 copy-start
  0.7 0.9 %copy-done = bf16[16,24,256]{2,1,0:T(8,128)(2,1)S(1)} copy-done((bf16[16,24,256]{2,1,0:T(8,128)(2,1)S(1)}, bf16[16,24,256]{2,1,0:T(8,128)(2,1)}, u32[]{:S(2)}) %copy-start) | copy-done | bytes 196632
  1.6 0.0 copy-start.1
  1.6 0.9 %copy-done.1 = bf16[256,256]{1,0:T(8,128)(2,1)S(1)} copy-done((bf16[256,256]{1,0:T(8,128)(2,1)S(1)}, bf16[256,256]{1,0:T(8,128)(2,1)}, u32[]{:S(2)}) %copy-start.1) | copy-done | bytes 131096
  2.5 0.0 copy-start.2
  2.5 0.9 %copy-done.2 = bf16[256,256]{1,0:T(8,128)(2,1)S(1)} copy-done((bf16[256,256]{1,0:T(8,128)(2,1)S(1)}, bf16[256,256]{1,0:T(8,128)(2,1)}, u32[]{:S(2)}) %copy-start.2) | copy-done | bytes 131096
  3.4 0.0 copy-start.3
  3.4 0.9 %copy-done.3 = bf16[256,3,2,32]{0,3,2,1:T(8,128)(2,1)S(1)} copy-done((bf16[256,3,2,32]{0,3,2,1:T(8,128)(2,1)S(1)}, bf16[256,3,2,32]{0,3,2,1:T(8,128)(2,1)}, u32[]{:S(2)}) %copy-start.3) | copy-done | bytes 98328
  4.3 0.0 copy-start.4
  4.3 0.8 %copy-done.4 = bf16[2,32,256]{2,1,0:T(8,128)(2,1)S(1)} copy-done((bf16[2,32,256]{2,1,0:T(8,128)(2,1)S(1)}, bf16[2,32,256]{2,1,0:T(8,128)(2,1)}, u32[]{:S(2)}) %copy-start.4) | copy-done | bytes 32792
  5.1 0.0 copy-start.5
  5.1 0.7 %copy-done.5 = bf16[7,7,256]{2,1,0:T(8,128)(2,1)S(1)} copy-done((bf16[7,7,256]{2,1,0:T(8,128)(2,1)S(1)}, bf16[7,7,256]{2,1,0:T(8,128)(2,1)}, u32[]{:S(2)}) %copy-start.5) | copy-done | bytes 25112
  5.8 0.0 copy-start.6
  5.8 0.7 %copy-done.6 = s32[16,256]{1,0:T(8,128)S(1)} copy-done((s32[16,256]{1,0:T(8,128)S(1)}, s32[16,256]{1,0:T(8,128)}, u32[]{:S(2)}) %copy-start.6) | copy-done | bytes 16408
  6.6 0.0 copy-start.7
  6.6 0.7 %copy-done.7 = s32[16,256]{1,0:T(8,128)S(1)} copy-done((s32[16,256]{1,0:T(8,128)S(1)}, s32[16,256]{1,0:T(8,128)}, u32[]{:S(2)}) %copy-start.7) | copy-done | bytes 16408
  7.3 48.9 %shard_map.109 = bf16[16,24,256]{2,1,0:T(8,128)(2,1)S(1)} custom-call(bf16[16,24,256]{2,1,0:T(8,128)(2,1)S(1)} %copy-done, f32[1,256]{1,0:T(1,128)S(1)} %bitcast.4, bf16[3,2,32,256]{3,2,1,0:T(8,128)(2,1)S(1)} %bitcast.3, f32[2]{0:T(128)S(1)} %copy-done.10, bf16[2,32,256]{2,1,0:T(8,128)(2,1)S(1)} %copy-done.4, s32[16,256]{1,0:T(8,128)S(1)} %copy-done.6, ...), custom_call_target="tpu_custom_call" | custom-call | tf_op jit(solution)/shard_map/pallas_call | solution.py:400
  56.2 0.7 %copy.13 = bf16[16,24,256]{2,1,0:T(8,128)(2,1)} copy(bf16[16,24,256]{2,1,0:T(8,128)(2,1)S(1)} %shard_map.109) | data formatting | bytes 393216
Async XLA Ops:
  0.0 0.7 %copy-start.9 = (f32[256]{0:T(256)S(1)}, f32[256]{0:T(256)}, u32[]{:S(2)}) copy-start(f32[256]{0:T(256)} %param.18) | copy-start | bytes 3076
  0.0 0.7 %copy-start.8 = (f32[256]{0:T(256)S(1)}, f32[256]{0:T(256)}, u32[]{:S(2)}) copy-start(f32[256]{0:T(256)} %param.12) | copy-start | bytes 3076
  0.0 0.7 %copy-start.10 = (f32[2]{0:T(128)S(1)}, f32[2]{0:T(128)}, u32[]{:S(2)}) copy-start(f32[2]{0:T(128)} %logit_scale.1) | copy-start | bytes 28
  0.7 0.9 %copy-start = (bf16[16,24,256]{2,1,0:T(8,128)(2,1)S(1)}, bf16[16,24,256]{2,1,0:T(8,128)(2,1)}, u32[]{:S(2)}) copy-start(bf16[16,24,256]{2,1,0:T(8,128)(2,1)} %fields.1) | copy-start | bytes 589828
  1.6 0.9 %copy-start.1 = (bf16[256,256]{1,0:T(8,128)(2,1)S(1)}, bf16[256,256]{1,0:T(8,128)(2,1)}, u32[]{:S(2)}) copy-start(bf16[256,256]{1,0:T(8,128)(2,1)} %w_up.1) | copy-start | bytes 393220
  2.5 0.9 %copy-start.2 = (bf16[256,256]{1,0:T(8,128)(2,1)S(1)}, bf16[256,256]{1,0:T(8,128)(2,1)}, u32[]{:S(2)}) copy-start(bf16[256,256]{1,0:T(8,128)(2,1)} %w_down.1) | copy-start | bytes 393220
  3.4 0.9 %copy-start.3 = (bf16[256,3,2,32]{0,3,2,1:T(8,128)(2,1)S(1)}, bf16[256,3,2,32]{0,3,2,1:T(8,128)(2,1)}, u32[]{:S(2)}) copy-start(bf16[256,3,2,32]{0,3,2,1:T(8,128)(2,1)} %param.13) | copy-start | bytes 294916
  4.3 0.8 %copy-start.4 = (bf16[2,32,256]{2,1,0:T(8,128)(2,1)S(1)}, bf16[2,32,256]{2,1,0:T(8,128)(2,1)}, u32[]{:S(2)}) copy-start(bf16[2,32,256]{2,1,0:T(8,128)(2,1)} %w_out.1) | copy-start | bytes 98308
  5.1 0.7 %copy-start.5 = (bf16[7,7,256]{2,1,0:T(8,128)(2,1)S(1)}, bf16[7,7,256]{2,1,0:T(8,128)(2,1)}, u32[]{:S(2)}) copy-start(bf16[7,7,256]{2,1,0:T(8,128)(2,1)} %dw_kernel.1) | copy-start | bytes 75268
  5.8 0.7 %copy-start.6 = (s32[16,256]{1,0:T(8,128)S(1)}, s32[16,256]{1,0:T(8,128)}, u32[]{:S(2)}) copy-start(s32[16,256]{1,0:T(8,128)} %attn_keep.1) | copy-start | bytes 49156
  6.6 0.7 %copy-start.7 = (s32[16,256]{1,0:T(8,128)S(1)}, s32[16,256]{1,0:T(8,128)}, u32[]{:S(2)}) copy-start(s32[16,256]{1,0:T(8,128)} %mlp_keep.1) | copy-start | bytes 49156

commit v2 on v1

--- a/solution.py
+++ b/solution.py
@@ -28,18 +28,26 @@
     n_lat,
     n_lon,
     n_ten,
+    fields_hbm,
+    gain1_hbm,
+    w_qkv_hbm,
+    logit_scale_hbm,
+    w_out,
+    attn_keep_hbm,
+    dw_kernel_hbm,
+    gain2_hbm,
+    w_up,
+    w_down,
+    mlp_keep_hbm,
+    out,
     fields,
     gain1,
     w_qkv,
     logit_scale,
-    w_out,
     attn_keep,
     dw_kernel,
     gain2,
-    w_up,
-    w_down,
     mlp_keep,
-    out,
     proj_w,
     sent,
     got,
@@ -53,7 +61,9 @@
     taps,
     ext,
     ext_f,
+    side,
     done,
+    fetch_sem,
     go_sem,
     send_a,
     recv_a,
@@ -62,6 +72,10 @@
     recv_b,
     send_w,
     recv_w,
+    send_p,
+    recv_p,
+    send_s,
+    recv_s,
     own_w,
     send_h,
     recv_h,
@@ -82,11 +96,20 @@
     lat = lax.axis_index("lat")
     lon = lax.axis_index("lon")
     ten = lax.axis_index("tensor")
-    band = lat * n_ten + ten
+    core = lax.rem(lat, 2)
+    sibling = {"lat": lat + 1 - 2 * core}
+
+    def turned(which_lat, place):
+        odd = lax.rem(which_lat, 2)
+        return place + odd * (n_ten - 1 - 2 * place)
+
+    part = turned(lat, ten)
+    band = lat * n_ten + part
 
     def band_at(step):
         there = lax.rem(band + step + bands, bands)
-        return {"lat": there // n_ten, "tensor": lax.rem(there, n_ten)}
+        there_lat = there // n_ten
+        return {"lat": there_lat, "tensor": turned(there_lat, lax.rem(there, n_ten))}
 
     def lon_at(step):
         return lax.rem(lon + step + n_lon, n_lon)
@@ -96,6 +119,24 @@
 
     def far_first(i):
         return n_lon // 2 + ((i + 1) // 2) * (1 - 2 * lax.rem(i, 2))
+
+    fetches = [
+        pltpu.make_async_copy(source, target, fetch_sem.at[index])
+        for index, (source, target) in enumerate(
+            (
+                (fields_hbm, fields),
+                (w_qkv_hbm, w_qkv),
+                (gain1_hbm, gain1),
+                (dw_kernel_hbm, dw_kernel),
+                (logit_scale_hbm, logit_scale),
+                (attn_keep_hbm, attn_keep),
+                (gain2_hbm, gain2),
+                (mlp_keep_hbm, mlp_keep),
+            )
+        )
+    ]
+    for fetch in fetches[:3]:
+        fetch.start()
 
     barrier = pltpu.get_barrier_semaphore()
 
@@ -112,8 +153,14 @@
         )
     for step in (-1, 1):
         pl.semaphore_signal(barrier, inc=1, device_id=band_at(step), device_id_type=MESH)
+    pl.semaphore_signal(barrier, inc=1, device_id=sibling, device_id_type=MESH)
+
+    for fetch in fetches[3:]:
+        fetch.start()
 
     proj_w[...] = jnp.zeros_like(proj_w)
+    for fetch in fetches[:3]:
+        fetch.wait()
     for head in range(heads):
         for which in range(3):
             proj_w[pl.ds(head * LANES + which * head_size, head_size), :] = w_qkv[which, head]
@@ -124,9 +171,10 @@
     projected = projected.reshape(rows, groups, SUB, heads * LANES)
     for row in range(rows):
         for head in range(heads):
-            sent[row * heads + head] = projected[row, :, :, head * LANES : (head + 1) * LANES]
-
-    pl.semaphore_wait(barrier, n_lon - 1 + n_ten - 1 + 2)
+            place = row % quarter * n_ten + row // quarter
+            sent[place * heads + head] = projected[row, :, :, head * LANES : (head + 1) * LANES]
+
+    pl.semaphore_wait(barrier, n_lon - 1 + n_ten - 1 + 3)
 
     def send_pair(i, carry):
         peer = lon_at(far_first(i))
@@ -150,13 +198,17 @@
     for step in (-1, 1):
         pl.semaphore_signal(go_sem, inc=1, device_id=band_at(step), device_id_type=MESH)
 
+    def half_of(ref):
+        half = ref.shape[0] // 2
+        return ref.at[pl.ds(core * half, half)]
+
     pairs_w = ((w_out, out_w), (w_up, up_w), (w_down, down_w))
-    weight_copies = []
+    weight_copies, weight_passes, weight_own = [], [], []
     for kind, (mine, whole) in enumerate(pairs_w):
         for step in range(1, n_ten):
             copy = pltpu.make_async_remote_copy(
-                src_ref=mine,
-                dst_ref=whole.at[ten],
+                src_ref=half_of(mine),
+                dst_ref=half_of(whole.at[ten]),
                 send_sem=send_w.at[kind, step - 1],
                 recv_sem=recv_w.at[kind, step - 1],
                 device_id={"tensor": ten_at(step)},
@@ -164,8 +216,42 @@
             )
             copy.start()
             weight_copies.append(copy)
-        pltpu.make_async_copy(mine, whole.at[ten], own_w.at[kind]).start()
-
+            arrived = half_of(whole.at[ten_at(n_ten - step)])
+            weight_passes.append(
+                pltpu.make_async_remote_copy(
+                    src_ref=arrived,
+                    dst_ref=arrived,
+                    send_sem=send_p.at[kind, step - 1],
+                    recv_sem=recv_p.at[kind, step - 1],
+                    device_id=sibling,
+                    device_id_type=MESH,
+                )
+            )
+        own = pltpu.make_async_copy(mine, whole.at[ten], own_w.at[kind])
+        own.start()
+        weight_own.append(own)
+
+    def weights_here(kind):
+        weight_own[kind].wait()
+        for step in range(1, n_ten):
+            weight_passes[kind * (n_ten - 1) + step - 1].wait_recv()
+
+    own_part = pl.ds(part * quarter, quarter)
+    side_copies = []
+    for index, (step, start) in enumerate(((1, cols - SUB), (-1, 0))):
+        copy = pltpu.make_async_remote_copy(
+            src_ref=fields.at[own_part, pl.ds(start, SUB)],
+            dst_ref=side.at[index],
+            send_sem=send_s.at[index],
+            recv_sem=recv_s.at[index],
+            device_id={"lon": lon_at(step)},
+            device_id_type=MESH,
+        )
+        copy.start()
+        side_copies.append(copy)
+
+    for fetch in fetches[3:]:
+        fetch.wait()
     for row_off in range(size):
         line = dw_kernel[row_off].astype(f32)
         for col_off in range(size):
@@ -176,31 +262,40 @@
                 )
 
     pltpu.make_async_copy(got, got, recv_a).wait()
+    for copy, onward in zip(weight_copies, weight_passes):
+        copy.wait_recv()
+        onward.start()
     keys = groups * n_lon * SUB
     gathered = got[...].reshape(keys, LANES)
     wide = gathered.astype(f32)
     lane = lax.broadcasted_iota(jnp.int32, (keys, LANES), 1)
     at_keys = (lane >= head_size) & (lane < 2 * head_size)
-    queries = jnp.where(at_keys, pltpu.roll(wide, head_size, 1), 0.0).astype(bf16)
-    for group in range(groups):
+    queries = jnp.where(at_keys, pltpu.roll(wide, head_size, 1), 0.0)
+    by_group = queries.reshape(groups, n_lon, SUB, LANES)
+    left_side = jnp.concatenate([by_group[-1, -1:], by_group[-1, :-1]], axis=0)
+    right_side = jnp.concatenate([by_group[0, 1:], by_group[0, :1]], axis=0)
+    place = lax.broadcasted_iota(jnp.int32, left_side.shape, 1)
+    beside = jnp.where(place >= SUB // 2, left_side, right_side)
+    span = n_lon * SUB
+    queries = [by_group[group].reshape(span, LANES).astype(bf16) for group in range(groups)]
+    queries.append(beside.reshape(span, LANES).astype(bf16))
+    for group in range(groups + 1):
         low, high = group * head_size, (group + 1) * head_size
         shift = (low - 2 * head_size) % LANES
         moved = pltpu.roll(wide, shift, 1) if shift else wide
         inside = (lane >= low) & (lane < high)
-        last = LANES if group == groups - 1 else high
         values[group, :, :LANES] = jnp.where(inside, moved, 0.0).astype(bf16)
-        values[group, :, LANES:] = jnp.where((lane >= low) & (lane < last), 1.0, 0.0).astype(bf16)
+        values[group, :, LANES:] = jnp.where(inside, 1.0, 0.0).astype(bf16)
     pair_head = lax.rem(lon, heads)
-    pair_row = lon // heads
+    pair_place = lon // heads
     scale = logit_scale[0]
     for head in range(1, heads):
         scale = jnp.where(pair_head == head, logit_scale[head], scale)
     coef = scale * (math.log2(math.e) / math.sqrt(head_size))
-    span = n_lon * SUB
     total = jnp.zeros((span, 2 * LANES), f32)
-    for group in range(groups):
+    for group in range(groups + 1):
         scores = lax.dot_general(
-            queries[group * span : (group + 1) * span],
+            queries[group],
             gathered,
             (((1,), (1,)), ((), ())),
             preferred_element_type=f32,
@@ -212,8 +307,8 @@
         (total[:, :LANES] / total[:, LANES:]).astype(bf16).reshape(n_lon, SUB, LANES)
     )
 
-    owner = pair_row // quarter
-    slot_row = lax.rem(pair_row, quarter)
+    owner = turned(lat, lax.rem(pair_place, n_ten))
+    slot_row = pair_place // n_ten
     slot_head = ten * heads + pair_head
     pl.semaphore_wait(go_sem, n_ten - 1 + 2)
 
@@ -249,12 +344,10 @@
         own_back.start()
 
     out_wide[...] = jnp.zeros_like(out_wide)
-    pltpu.make_async_copy(w_out, out_w.at[ten], own_w.at[0]).wait()
-    for step in range(1, n_ten):
-        weight_copies[step - 1].wait_recv()
+    weights_here(0)
     for head in range(all_heads):
         block = out_w[head // heads, head % heads]
-        for group in range(groups):
+        for group in range(groups + 1):
             out_wide[
                 pl.ds(head * LANES + group * head_size, head_size),
                 pl.ds(group * channels, channels),
@@ -265,53 +358,45 @@
         [joined[:, head].reshape(quarter * SUB, LANES) for head in range(all_heads)], axis=-1
     )
     attended = jnp.dot(packed, out_wide[...], preferred_element_type=f32)
+    for copy in side_copies:
+        copy.wait_recv()
+    place = lax.broadcasted_iota(jnp.int32, (SUB, channels), 0)
     for row in range(quarter):
-        at = ten * quarter + row
+        at = part * quarter + row
         factor = attn_keep[pl.ds(at, 1), :].astype(f32) / keep_prob
         block = fields[at].astype(f32)
-        for group in range(groups):
+        for group in range(groups + 1):
             piece = attended[
                 row * SUB : (row + 1) * SUB, group * channels : (group + 1) * channels
             ]
-            ext[margin + row, pl.ds((group + 1) * SUB, SUB), :] = (
-                block[group * SUB : (group + 1) * SUB] + piece * factor
-            ).astype(bf16)
-
-    first, final = pl.ds(SUB, SUB), pl.ds(cols, SUB)
-    left, right, middle = pl.ds(0, SUB), pl.ds(cols + SUB, SUB), pl.ds(SUB, cols)
-    top_rows, low_rows = pl.ds(margin, margin), pl.ds(quarter, margin)
-    above, below, own_rows = (
-        pl.ds(0, margin),
-        pl.ds(margin + quarter, margin),
-        pl.ds(margin, quarter),
-    )
+            if group < groups:
+                base = block[group * SUB : (group + 1) * SUB]
+            else:
+                base = jnp.where(
+                    place >= SUB // 2, side[0, row].astype(f32), side[1, row].astype(f32)
+                )
+            stream = (base + piece * factor).astype(bf16)
+            if group < groups:
+                ext[margin + row, pl.ds((group + 1) * SUB, SUB), :] = stream
+            else:
+                ext[margin + row, pl.ds(0, SUB), :] = stream
+                ext[margin + row, pl.ds(cols + SUB, SUB), :] = stream
+
+    middle = pl.ds(SUB, cols)
     halo_copies = []
-    for band_step, src_rows, dst_rows in (
-        (-1, top_rows, below),
-        (1, low_rows, above),
-        (0, own_rows, own_rows),
+    for index, (step, source, target) in enumerate(
+        ((-1, margin, margin + quarter), (1, quarter, 0))
     ):
-        for lon_step, src_cols, dst_cols in (
-            (-1, first, right),
-            (1, final, left),
-            (0, middle, middle),
-        ):
-            if band_step == 0 and lon_step == 0:
-                continue
-            where = dict(band_at(band_step)) if band_step else {}
-            if lon_step:
-                where["lon"] = lon_at(lon_step)
-            index = len(halo_copies)
-            copy = pltpu.make_async_remote_copy(
-                src_ref=ext.at[src_rows, src_cols],
-                dst_ref=ext.at[dst_rows, dst_cols],
-                send_sem=send_h.at[index],
-                recv_sem=recv_h.at[index],
-                device_id=where,
-                device_id_type=MESH,
-            )
-            copy.start()
-            halo_copies.append(copy)
+        copy = pltpu.make_async_remote_copy(
+            src_ref=ext.at[pl.ds(source, margin)],
+            dst_ref=ext.at[pl.ds(target, margin)],
+            send_sem=send_h.at[index],
+            recv_sem=recv_h.at[index],
+            device_id=band_at(step),
+            device_id_type=MESH,
+        )
+        copy.start()
+        halo_copies.append(copy)
     for copy in halo_copies:
         copy.wait_recv()
 
@@ -340,27 +425,23 @@
     spatial = jnp.concatenate(parts, axis=-1).astype(bf16).astype(f32)
 
     normed2 = layer_norm(spatial, gain2[...])
-    for kind in (1, 2):
-        mine, whole = pairs_w[kind]
-        pltpu.make_async_copy(mine, whole.at[ten], own_w.at[kind]).wait()
-        for step in range(1, n_ten):
-            weight_copies[kind * (n_ten - 1) + step - 1].wait_recv()
+    weights_here(1)
+    weights_here(2)
     ffn = jnp.zeros((quarter * cols, channels), f32)
-    for part in range(n_ten):
-        inner = jnp.dot(normed2, up_w[part], preferred_element_type=f32)
+    for index in range(n_ten):
+        inner = jnp.dot(normed2, up_w[index], preferred_element_type=f32)
         hidden = (0.5 * inner * (1.0 + lax.erf(inner * math.sqrt(0.5)))).astype(bf16)
-        ffn = ffn + jnp.dot(hidden, down_w[part], preferred_element_type=f32)
+        ffn = ffn + jnp.dot(hidden, down_w[index], preferred_element_type=f32)
     for row in range(quarter):
-        factor = mlp_keep[pl.ds(ten * quarter + row, 1), :].astype(f32) / keep_prob
+        factor = mlp_keep[pl.ds(part * quarter + row, 1), :].astype(f32) / keep_prob
         stream = ext[margin + row, middle, :].astype(f32)
         done[row] = (stream + ffn[row * cols : (row + 1) * cols] * factor).astype(bf16)
 
-    mine = pl.ds(ten * quarter, quarter)
     out_copies = []
     for step in range(1, n_ten):
         copy = pltpu.make_async_remote_copy(
             src_ref=done,
-            dst_ref=out.at[mine],
+            dst_ref=out.at[own_part],
             send_sem=send_o.at[step - 1],
             recv_sem=recv_o.at[step - 1],
             device_id={"tensor": ten_at(step)},
@@ -368,7 +449,7 @@
         )
         copy.start()
         out_copies.append(copy)
-    own_out = pltpu.make_async_copy(done, out.at[mine], send_o.at[n_ten - 1])
+    own_out = pltpu.make_async_copy(done, out.at[own_part], send_o.at[n_ten - 1])
     own_out.start()
 
     pltpu.make_async_copy(sent.at[: n_lon - 1], sent.at[: n_lon - 1], send_a).wait()
@@ -378,7 +459,7 @@
     def _():
         own_back.wait_send()
 
-    for copy in weight_copies + halo_copies + out_copies:
+    for copy in weight_copies + weight_passes + side_copies + halo_copies + out_copies:
         copy.wait_send()
     own_out.wait()
     for copy in out_copies:
@@ -393,55 +474,72 @@
     groups, quarter, size = cols // SUB, rows // n_ten, dw_kernel.shape[0]
     margin, halves = size // 2, channels // LANES
     span = quarter + 2 * margin
-    vmem = pl.BlockSpec(memory_space=pltpu.VMEM)
-    hbm = pl.BlockSpec(memory_space=pl.ANY)
-    smem = pl.BlockSpec(memory_space=pltpu.SMEM)
+    hbm = pl.BlockSpec(memory_space=pltpu.HBM)
     dma = pltpu.SemaphoreType.DMA
     return pl.pallas_call(
         functools.partial(kernel, n_lat, n_lon, n_ten),
         out_shape=jax.ShapeDtypeStruct(fields.shape, bf16),
-        in_specs=[vmem, vmem, vmem, smem, hbm, vmem, vmem, vmem, hbm, hbm, vmem],
-        out_specs=hbm,
+        in_specs=[hbm] * 11,
+        out_specs=pl.BlockSpec(memory_space=pl.ANY),
         scratch_shapes=[
+            pltpu.VMEM(fields.shape, bf16),
+            pltpu.VMEM((1, channels), f32),
+            pltpu.VMEM((3, heads, head_size, channels), bf16),
+            pltpu.SMEM(logit_scale.shape, f32),
+            pltpu.VMEM(attn_keep.shape, jnp.int32),
+            pltpu.VMEM(dw_kernel.shape, bf16),
+            pltpu.VMEM((1, channels), f32),
+            pltpu.VMEM(mlp_keep.shape, jnp.int32),
             pltpu.VMEM((heads * LANES, channels), bf16),
             pltpu.VMEM((n_lon, groups, SUB, LANES), bf16),
             pltpu.VMEM((groups, n_lon, SUB, LANES), bf16),
-            pltpu.VMEM((groups, groups * n_lon * SUB, 2 * LANES), bf16),
+            pltpu.VMEM((groups + 1, groups * n_lon * SUB, 2 * LANES), bf16),
             pltpu.VMEM((n_lon, SUB, LANES), bf16),
             pltpu.VMEM((quarter, heads * n_ten, SUB, LANES), bf16),
             pltpu.VMEM((n_ten,) + w_out.shape, bf16),
-            pltpu.VMEM((heads * n_ten * LANES, groups * channels), bf16),
+            pltpu.VMEM((heads * n_ten * LANES, (groups + 1) * channels), bf16),
             pltpu.VMEM((n_ten, channels, hidden), bf16),
             pltpu.VMEM((n_ten, hidden, channels), bf16),
             pltpu.VMEM((halves, size * size, SUB, LANES), f32),
             pltpu.VMEM((span, cols + 2 * SUB, channels), bf16),
             pltpu.VMEM((halves, span, cols + 2 * SUB, LANES), f32),
+            pltpu.VMEM((2, quarter, SUB, channels), bf16),
             pltpu.VMEM((quarter, cols, channels), bf16),
+            dma((8,)),
             pltpu.SemaphoreType.REGULAR,
             dma, dma, dma, dma, dma,
             dma((3, n_ten - 1)),
             dma((3, n_ten - 1)),
+            dma((3, n_ten - 1)),
+            dma((3, n_ten - 1)),
+            dma((2,)),
+            dma((2,)),
             dma((3,)),
-            dma((8,)),
-            dma((8,)),
+            dma((2,)),
+            dma((2,)),
             dma((n_ten,)),
             dma((n_ten - 1,)),
         ],
         compiler_params=pltpu.CompilerParams(
-            collective_id=0, has_side_effects=True, vmem_limit_bytes=48 << 20
+            collective_id=0, has_side_effects=True, vmem_limit_bytes=56 << 20
         ),
     )(
-        fields,
-        gain1.reshape(1, channels),
-        w_qkv.transpose(1, 2, 3, 0),
-        logit_scale,
-        w_out,
-        attn_keep,
-        dw_kernel,
-        gain2.reshape(1, channels),
-        w_up,
-        w_down,
-        mlp_keep,
+        *(
+            pltpu.with_memory_space_constraint(operand, pltpu.HBM)
+            for operand in (
+                fields,
+                gain1.reshape(1, channels),
+                w_qkv.transpose(1, 2, 3, 0),
+                logit_scale,
+                w_out,
+                attn_keep,
+                dw_kernel,
+                gain2.reshape(1, channels),
+                w_up,
+                w_down,
+                mlp_keep,
+            )
+        )
     )
 
 

time: 57.3 us -> 49.6 us (0.87)
  the two profiles are of different devices: /device:TPU:4 before, /device:TPU:1 now
where the time goes in v2:
time: 49.6 us; the launch traced here: 49.5 us
  Pallas kernels  47.8 us (96%)
  local copies, waits for them, and re-layouts  1.62 us (3%)
    pallas_call x1, Pallas kernels, shards(): pl.pallas_call(functools.partial(kernel, n_lat, n_lon, n_ten), out_shape=...  47.8 us
    unnamed x1, local copies, waits for them, and re-layouts  1.62 us

profile of v2, /device:TPU:1, one launch (start us, length us, event | category | flops | bytes accessed | tf_op | source)
XLA Modules:
  0.0 49.5 jit_solution(16361493121893311918)
XLA Ops:
  0.0 47.8 %shard_map.109 = bf16[16,24,256]{2,1,0:T(8,128)(2,1)} custom-call(bf16[16,24,256]{2,1,0:T(8,128)(2,1)} %fields_hbm.1, f32[1,256]{1,0:T(1,128)} %bitcast.4, bf16[3,2,32,256]{3,2,1,0:T(8,128)(2,1)} %bitcast.3, f32[2]{0:T(128)} %logit_scale_hbm.1, bf16[2,32,256]{2,1,0:T(8,128)(2,1)} %w_out.1, s32[16,256]{1,0:T(8,128)} %attn_keep_hbm.1, ...), custom_call_target="tpu_custom_call" | custom-call | tf_op jit(solution)/shard_map/pallas_call | solution.py:479
  47.8 1.6 %copy.13 = bf16[16,24,256]{2,1,0:T(8,128)(2,1)} copy(bf16[16,24,256]{2,1,0:T(8,128)(2,1)} %shard_map.109) | data formatting | bytes 393216

commit v3 on v2

--- a/solution.py
+++ b/solution.py
@@ -92,6 +92,8 @@
     margin = size // 2
     halves = channels // LANES
     bands = n_lat * n_ten
+    spot_of = (14, 1, 15, 0, 8, 7, 9, 6, 10, 5, 11, 4, 12, 3, 13, 2)
+    row_of = (3, 1, 15, 13, 11, 9, 7, 5, 4, 6, 8, 10, 12, 14, 0, 2)
 
     lat = lax.axis_index("lat")
     lon = lax.axis_index("lon")
@@ -119,6 +121,9 @@
 
     def far_first(i):
         return n_lon // 2 + ((i + 1) // 2) * (1 - 2 * lax.rem(i, 2))
+
+    def by_core(i):
+        return far_first(i + core * (n_lon - 2 - 2 * i))
 
     fetches = [
         pltpu.make_async_copy(source, target, fetch_sem.at[index])
@@ -171,13 +176,13 @@
     projected = projected.reshape(rows, groups, SUB, heads * LANES)
     for row in range(rows):
         for head in range(heads):
-            place = row % quarter * n_ten + row // quarter
+            place = spot_of[row]
             sent[place * heads + head] = projected[row, :, :, head * LANES : (head + 1) * LANES]
 
     pl.semaphore_wait(barrier, n_lon - 1 + n_ten - 1 + 3)
 
     def send_pair(i, carry):
-        peer = lon_at(far_first(i))
+        peer = lon_at(by_core(i))
         pltpu.make_async_remote_copy(
             src_ref=sent.at[peer],
             dst_ref=got.at[:, lon],
@@ -307,8 +312,11 @@
         (total[:, :LANES] / total[:, LANES:]).astype(bf16).reshape(n_lon, SUB, LANES)
     )
 
-    owner = turned(lat, lax.rem(pair_place, n_ten))
-    slot_row = pair_place // n_ten
+    pair_row = row_of[0]
+    for index in range(1, rows):
+        pair_row = jnp.where(pair_place == index, row_of[index], pair_row)
+    owner = turned(lat, pair_row // quarter)
+    slot_row = lax.rem(pair_row, quarter)
     slot_head = ten * heads + pair_head
     pl.semaphore_wait(go_sem, n_ten - 1 + 2)
 
@@ -380,7 +388,6 @@
                 ext[margin + row, pl.ds((group + 1) * SUB, SUB), :] = stream
             else:
                 ext[margin + row, pl.ds(0, SUB), :] = stream
-                ext[margin + row, pl.ds(cols + SUB, SUB), :] = stream
 
     middle = pl.ds(SUB, cols)
     halo_copies = []
@@ -395,19 +402,39 @@
             device_id=band_at(step),
             device_id_type=MESH,
         )
-        copy.start()
         halo_copies.append(copy)
-    for copy in halo_copies:
-        copy.wait_recv()
+    has_above, has_below = band > 0, band < bands - 1
+
+    @pl.when(has_above)
+    def _():
+        halo_copies[0].start()
+
+    @pl.when(has_below)
+    def _():
+        halo_copies[1].start()
+
+    @pl.when(jnp.logical_not(has_above))
+    def _():
+        ext[pl.ds(0, margin)] = jnp.zeros((margin,) + ext.shape[1:], bf16)
+
+    @pl.when(jnp.logical_not(has_below))
+    def _():
+        ext[pl.ds(margin + quarter, margin)] = jnp.zeros((margin,) + ext.shape[1:], bf16)
+
+    @pl.when(has_above)
+    def _():
+        halo_copies[1].wait_recv()
+
+    @pl.when(has_below)
+    def _():
+        halo_copies[0].wait_recv()
 
     for row in range(quarter + 2 * margin):
         line = ext[row].astype(f32)
-        if row < margin:
-            line = jnp.where(band > 0, line, 0.0)
-        if row >= margin + quarter:
-            line = jnp.where(band < bands - 1, line, 0.0)
         for half in range(halves):
-            ext_f[half, row] = line[:, half * LANES : (half + 1) * LANES]
+            piece = line[:, half * LANES : (half + 1) * LANES]
+            ext_f[half, row, pl.ds(0, cols + SUB), :] = piece
+            ext_f[half, row, pl.ds(cols + SUB, SUB), :] = piece[:SUB]
     parts = []
     for half in range(halves):
         sums = [jnp.zeros((cols, LANES), f32) for _ in range(quarter)]
@@ -438,13 +465,15 @@
         done[row] = (stream + ffn[row * cols : (row + 1) * cols] * factor).astype(bf16)
 
     out_copies = []
-    for step in range(1, n_ten):
+    for index in range(n_ten - 1):
+        target = index + (index >= ten).astype(jnp.int32)
+        slot = lax.rem(target - ten + n_ten - 1, n_ten)
         copy = pltpu.make_async_remote_copy(
             src_ref=done,
             dst_ref=out.at[own_part],
-            send_sem=send_o.at[step - 1],
-            recv_sem=recv_o.at[step - 1],
-            device_id={"tensor": ten_at(step)},
+            send_sem=send_o.at[index],
+            recv_sem=recv_o.at[slot],
+            device_id={"tensor": target},
             device_id_type=MESH,
         )
         copy.start()
@@ -452,6 +481,14 @@
     own_out = pltpu.make_async_copy(done, out.at[own_part], send_o.at[n_ten - 1])
     own_out.start()
 
+    @pl.when(has_above)
+    def _():
+        halo_copies[0].wait_send()
+
+    @pl.when(has_below)
+    def _():
+        halo_copies[1].wait_send()
+
     pltpu.make_async_copy(sent.at[: n_lon - 1], sent.at[: n_lon - 1], send_a).wait()
     pltpu.make_async_copy(mixed.at[: n_lon - 1], mixed.at[: n_lon - 1], send_b).wait()
 
@@ -459,11 +496,11 @@
     def _():
         own_back.wait_send()
 
-    for copy in weight_copies + weight_passes + side_copies + halo_copies + out_copies:
+    for copy in weight_copies + weight_passes + side_copies + out_copies:
         copy.wait_send()
     own_out.wait()
-    for copy in out_copies:
-        copy.wait_recv()
+    for slot in range(n_ten - 1):
+        pltpu.make_async_copy(done, out.at[own_part], recv_o.at[slot]).wait()
 
 
 def shards(sizes, fields, gain1, w_qkv, logit_scale, w_out, attn_keep, dw_kernel, gain2, w_up, w_down, mlp_keep):
@@ -501,7 +538,7 @@
             pltpu.VMEM((n_ten, channels, hidden), bf16),
             pltpu.VMEM((n_ten, hidden, channels), bf16),
             pltpu.VMEM((halves, size * size, SUB, LANES), f32),
-            pltpu.VMEM((span, cols + 2 * SUB, channels), bf16),
+            pltpu.VMEM((span, cols + SUB, channels), bf16),
             pltpu.VMEM((halves, span, cols + 2 * SUB, LANES), f32),
             pltpu.VMEM((2, quarter, SUB, channels), bf16),
             pltpu.VMEM((quarter, cols, channels), bf16),
@@ -521,7 +558,7 @@
             dma((n_ten - 1,)),
         ],
         compiler_params=pltpu.CompilerParams(
-            collective_id=0, has_side_effects=True, vmem_limit_bytes=56 << 20
+            collective_id=0, has_side_effects=True, vmem_limit_bytes=32 << 20
         ),
     )(
         *(

time: 49.6 us -> 47.9 us (0.966)
  the two profiles are of different devices: /device:TPU:1 before, /device:TPU:4 now
where the time goes in v3:
time: 47.9 us; the launch traced here: 47.7 us
  Pallas kernels  47 us (98%)
  local copies, waits for them, and re-layouts  0.68 us (1%)
    pallas_call x1, Pallas kernels, shards(): pl.pallas_call(functools.partial(kernel, n_lat, n_lon, n_ten), out_shape=...  47 us

profile of v3, /device:TPU:4, one launch (start us, length us, event | category | flops | bytes accessed | tf_op | source)
XLA Modules:
  0.0 47.7 jit_solution(14374751490666688933)
XLA Ops:
  0.0 47.0 %shard_map.109 = bf16[16,24,256]{2,1,0:T(8,128)(2,1)S(1)} custom-call(bf16[16,24,256]{2,1,0:T(8,128)(2,1)} %fields_hbm.1, f32[1,256]{1,0:T(1,128)} %bitcast.4, bf16[3,2,32,256]{3,2,1,0:T(8,128)(2,1)} %bitcast.3, f32[2]{0:T(128)} %logit_scale_hbm.1, bf16[2,32,256]{2,1,0:T(8,128)(2,1)} %w_out.1, s32[16,256]{1,0:T(8,128)} %attn_keep_hbm.1, ...), custom_call_target="tpu_custom_call" | custom-call | tf_op jit(solution)/shard_map/pallas_call | solution.py:516
  47.0 0.7 %copy.13 = bf16[16,24,256]{2,1,0:T(8,128)(2,1)} copy(bf16[16,24,256]{2,1,0:T(8,128)(2,1)S(1)} %shard_map.109) | data formatting | bytes 393216

commit v4 on v3

--- a/solution.py
+++ b/solution.py
@@ -267,9 +267,6 @@
                 )
 
     pltpu.make_async_copy(got, got, recv_a).wait()
-    for copy, onward in zip(weight_copies, weight_passes):
-        copy.wait_recv()
-        onward.start()
     keys = groups * n_lon * SUB
     gathered = got[...].reshape(keys, LANES)
     wide = gathered.astype(f32)
@@ -297,21 +294,6 @@
     for head in range(1, heads):
         scale = jnp.where(pair_head == head, logit_scale[head], scale)
     coef = scale * (math.log2(math.e) / math.sqrt(head_size))
-    total = jnp.zeros((span, 2 * LANES), f32)
-    for group in range(groups + 1):
-        scores = lax.dot_general(
-            queries[group],
-            gathered,
-            (((1,), (1,)), ((), ())),
-            preferred_element_type=f32,
-        )
-        top = jnp.max(scores, axis=-1, keepdims=True)
-        weights = jnp.exp2((scores - top) * coef).astype(bf16)
-        total = total + jnp.dot(weights, values[group], preferred_element_type=f32)
-    mixed[...] = (
-        (total[:, :LANES] / total[:, LANES:]).astype(bf16).reshape(n_lon, SUB, LANES)
-    )
-
     pair_row = row_of[0]
     for index in range(1, rows):
         pair_row = jnp.where(pair_place == index, row_of[index], pair_row)
@@ -320,19 +302,37 @@
     slot_head = ten * heads + pair_head
     pl.semaphore_wait(go_sem, n_ten - 1 + 2)
 
-    def send_back(i, carry):
-        peer = lon_at(far_first(i))
-        pltpu.make_async_remote_copy(
-            src_ref=mixed.at[peer],
-            dst_ref=joined.at[slot_row, slot_head],
-            send_sem=send_b,
-            recv_sem=recv_b,
-            device_id={"lon": peer, "tensor": owner},
-            device_id_type=MESH,
-        ).start()
+    def send_back(peer, carry):
+        @pl.when(peer != lon)
+        def _():
+            pltpu.make_async_remote_copy(
+                src_ref=mixed.at[peer],
+                dst_ref=joined.at[slot_row, slot_head],
+                send_sem=send_b,
+                recv_sem=recv_b,
+                device_id={"lon": peer, "tensor": owner},
+                device_id_type=MESH,
+            ).start()
+
         return carry
 
-    lax.fori_loop(0, n_lon - 1, send_back, 0)
+    portion = n_lon // 2
+    for start in range(0, n_lon, portion):
+        total = jnp.zeros((portion * SUB, 2 * LANES), f32)
+        for group in range(groups + 1):
+            scores = lax.dot_general(
+                queries[group][start * SUB : (start + portion) * SUB],
+                gathered,
+                (((1,), (1,)), ((), ())),
+                preferred_element_type=f32,
+            )
+            top = jnp.max(scores, axis=-1, keepdims=True)
+            weights = jnp.exp2((scores - top) * coef).astype(bf16)
+            total = total + jnp.dot(weights, values[group], preferred_element_type=f32)
+        mixed[pl.ds(start, portion)] = (
+            (total[:, :LANES] / total[:, LANES:]).astype(bf16).reshape(portion, SUB, LANES)
+        )
+        lax.fori_loop(start, start + portion, send_back, 0)
 
     @pl.when(owner == ten)
     def _():
@@ -350,6 +350,10 @@
     @pl.when(owner != ten)
     def _():
         own_back.start()
+
+    for copy, onward in zip(weight_copies, weight_passes):
+        copy.wait_recv()
+        onward.start()
 
     out_wide[...] = jnp.zeros_like(out_wide)
     weights_here(0)

time: 47.9 us -> 47.6 us (level)
  no operation moved by 1% of the time
where the time goes in v4:
time: 47.6 us; the launch traced here: 47.5 us
  Pallas kernels  46.8 us (98%)
  local copies, waits for them, and re-layouts  0.68 us (1%)
    pallas_call x1, Pallas kernels, shards(): pl.pallas_call(functools.partial(kernel, n_lat, n_lon, n_ten), out_shape=...  46.8 us

profile of v4, /device:TPU:4, one launch (start us, length us, event | category | flops | bytes accessed | tf_op | source)
XLA Modules:
  0.0 47.5 jit_solution(1645228352994173916)
XLA Ops:
  0.0 46.8 %shard_map.109 = bf16[16,24,256]{2,1,0:T(8,128)(2,1)S(1)} custom-call(bf16[16,24,256]{2,1,0:T(8,128)(2,1)} %fields_hbm.1, f32[1,256]{1,0:T(1,128)} %bitcast.4, bf16[3,2,32,256]{3,2,1,0:T(8,128)(2,1)} %bitcast.3, f32[2]{0:T(128)} %logit_scale_hbm.1, bf16[2,32,256]{2,1,0:T(8,128)(2,1)} %w_out.1, s32[16,256]{1,0:T(8,128)} %attn_keep_hbm.1, ...), custom_call_target="tpu_custom_call" | custom-call | tf_op jit(solution)/shard_map/pallas_call | solution.py:520
  46.8 0.7 %copy.13 = bf16[16,24,256]{2,1,0:T(8,128)(2,1)} copy(bf16[16,24,256]{2,1,0:T(8,128)(2,1)S(1)} %shard_map.109) | data formatting | bytes 393216

commit v5 on v4

--- a/solution.py
+++ b/solution.py
@@ -55,7 +55,6 @@
     mixed,
     joined,
     out_w,
-    out_wide,
     up_w,
     down_w,
     taps,
@@ -355,21 +354,29 @@
         copy.wait_recv()
         onward.start()
 
-    out_wide[...] = jnp.zeros_like(out_wide)
     weights_here(0)
-    for head in range(all_heads):
-        block = out_w[head // heads, head % heads]
-        for group in range(groups + 1):
-            out_wide[
-                pl.ds(head * LANES + group * head_size, head_size),
-                pl.ds(group * channels, channels),
-            ] = block
-
+    out_all = out_w[...].reshape(all_heads * head_size, channels)
+    lane = lax.broadcasted_iota(jnp.int32, (quarter * SUB, LANES), 1)
+    per_tile = LANES // head_size
     pltpu.make_async_copy(joined, joined, recv_b).wait()
-    packed = jnp.concatenate(
-        [joined[:, head].reshape(quarter * SUB, LANES) for head in range(all_heads)], axis=-1
+    tiles = [
+        joined[:, head].reshape(quarter * SUB, LANES).astype(f32) for head in range(all_heads)
+    ]
+    lines = []
+    for group in range(groups + 1):
+        line = []
+        for start in range(0, all_heads, per_tile):
+            merged = None
+            for k in range(per_tile):
+                shift = (k - group) * head_size % LANES
+                moved = tiles[start + k]
+                moved = pltpu.roll(moved, shift, 1) if shift else moved
+                merged = jnp.where(lane >= k * head_size, moved, merged) if k else moved
+            line.append(merged)
+        lines.append(jnp.concatenate(line, axis=-1))
+    attended = jnp.dot(
+        jnp.concatenate(lines, axis=0).astype(bf16), out_all, preferred_element_type=f32
     )
-    attended = jnp.dot(packed, out_wide[...], preferred_element_type=f32)
     for copy in side_copies:
         copy.wait_recv()
     place = lax.broadcasted_iota(jnp.int32, (SUB, channels), 0)
@@ -378,9 +385,8 @@
         factor = attn_keep[pl.ds(at, 1), :].astype(f32) / keep_prob
         block = fields[at].astype(f32)
         for group in range(groups + 1):
-            piece = attended[
-                row * SUB : (row + 1) * SUB, group * channels : (group + 1) * channels
-            ]
+            at_piece = (group * quarter + row) * SUB
+            piece = attended[at_piece : at_piece + SUB]
             if group < groups:
                 base = block[group * SUB : (group + 1) * SUB]
             else:
@@ -538,7 +544,6 @@
             pltpu.VMEM((n_lon, SUB, LANES), bf16),
             pltpu.VMEM((quarter, heads * n_ten, SUB, LANES), bf16),
             pltpu.VMEM((n_ten,) + w_out.shape, bf16),
-            pltpu.VMEM((heads * n_ten * LANES, (groups + 1) * channels), bf16),
             pltpu.VMEM((n_ten, channels, hidden), bf16),
             pltpu.VMEM((n_ten, hidden, channels), bf16),
             pltpu.VMEM((halves, size * size, SUB, LANES), f32),

time: 47.6 us -> 47.3 us (level)
  no operation moved by 1% of the time
where the time goes in v5:
time: 47.3 us; the launch traced here: 47.2 us
  Pallas kernels  46.5 us (98%)
  local copies, waits for them, and re-layouts  0.68 us (1%)
    pallas_call x1, Pallas kernels, shards(): pl.pallas_call(functools.partial(kernel, n_lat, n_lon, n_ten), out_shape=...  46.5 us

profile of v5, /device:TPU:4, one launch (start us, length us, event | category | flops | bytes accessed | tf_op | source)
XLA Modules:
  0.0 47.2 jit_solution(7528920132428652393)
XLA Ops:
  0.0 46.5 %shard_map.109 = bf16[16,24,256]{2,1,0:T(8,128)(2,1)S(1)} custom-call(bf16[16,24,256]{2,1,0:T(8,128)(2,1)} %fields_hbm.1, f32[1,256]{1,0:T(1,128)} %bitcast.4, bf16[3,2,32,256]{3,2,1,0:T(8,128)(2,1)} %bitcast.3, f32[2]{0:T(128)} %logit_scale_hbm.1, bf16[2,32,256]{2,1,0:T(8,128)(2,1)} %w_out.1, s32[16,256]{1,0:T(8,128)} %attn_keep_hbm.1, ...), custom_call_target="tpu_custom_call" | custom-call | tf_op jit(solution)/shard_map/pallas_call | solution.py:526
  46.5 0.7 %copy.13 = bf16[16,24,256]{2,1,0:T(8,128)(2,1)} copy(bf16[16,24,256]{2,1,0:T(8,128)(2,1)S(1)} %shard_map.109) | data formatting | bytes 393216

commit v6 on v5

--- a/solution.py
+++ b/solution.py
@@ -315,7 +315,7 @@
 
         return carry
 
-    portion = n_lon // 2
+    portion = n_lon // 4
     for start in range(0, n_lon, portion):
         total = jnp.zeros((portion * SUB, 2 * LANES), f32)
         for group in range(groups + 1):

time: 47.3 us -> 47.3 us (level)
  no operation moved by 1% of the time
where the time goes in v6:
time: 47.3 us; the launch traced here: 47.1 us
  Pallas kernels  46.4 us (98%)
  local copies, waits for them, and re-layouts  0.68 us (1%)
    pallas_call x1, Pallas kernels, shards(): pl.pallas_call(functools.partial(kernel, n_lat, n_lon, n_ten), out_shape=...  46.4 us

profile of v6, /device:TPU:4, one launch (start us, length us, event | category | flops | bytes accessed | tf_op | source)
XLA Modules:
  0.0 47.1 jit_solution(1319759919211513492)
XLA Ops:
  0.0 46.4 %shard_map.109 = bf16[16,24,256]{2,1,0:T(8,128)(2,1)S(1)} custom-call(bf16[16,24,256]{2,1,0:T(8,128)(2,1)} %fields_hbm.1, f32[1,256]{1,0:T(1,128)} %bitcast.4, bf16[3,2,32,256]{3,2,1,0:T(8,128)(2,1)} %bitcast.3, f32[2]{0:T(128)} %logit_scale_hbm.1, bf16[2,32,256]{2,1,0:T(8,128)(2,1)} %w_out.1, s32[16,256]{1,0:T(8,128)} %attn_keep_hbm.1, ...), custom_call_target="tpu_custom_call" | custom-call | tf_op jit(solution)/shard_map/pallas_call | solution.py:526
  46.4 0.7 %copy.13 = bf16[16,24,256]{2,1,0:T(8,128)(2,1)} copy(bf16[16,24,256]{2,1,0:T(8,128)(2,1)S(1)} %shard_map.109) | data formatting | bytes 393216
